TPU v7x, 512 devices: a whole 4x4x16 slice. The times are simulated.
512 devices in a mesh: seq: 128 (over y, z, x_lo), batch: 4 (over x_hi, core).
Axes of the slice: x: 4 (x_hi: 2, x_lo: 2; x = x_hi * 2 + x_lo), y: 4, z: 16, core: 2. Of those that a mesh axis runs over, the one named last changes fastest.
Arguments:
- tokens: bfloat16 [4, 262144, 256], P('batch', 'seq'), may hold values from -6 to 6
- cotangent: bfloat16 [4, 262144, 256], P('batch', 'seq'), may hold values from -3 to 3
- first_factor: bfloat16 [512, 512, 512], P('seq', 'batch'), may hold values from -0.25 to 0.25
- second_factor: bfloat16 [512, 512, 512], P('seq', 'batch'), may hold values from -0.25 to 0.25
- gate_source: int32 [256], replicated, may hold values from 0 to 255
- alternate: int32 [512], replicated, may hold values from 0 to 511, each once
Outputs:
- grad_tokens: bfloat16 [4, 262144, 256], P('batch', 'seq')
- grad_first: bfloat16 [512, 512, 512], P('seq', 'batch')
- grad_second: bfloat16 [512, 512, 512], P('seq', 'batch')
Inputs may be any that keep to these rules, and one draw needn't show every extreme that they name: `alternate`: a permutation: each of 0 to 511 once.
All inputs are finite; a program needn't handle non-finite values.
Results may differ from a plain program's by a relative error of at most 0.012.
Values may be sent and summed in bfloat16 or wider, within the bound.
A program may use at most 64 MiB of HBM per device.

v0:
```python
import jax
import jax.numpy as jnp
from jax import lax
from jax.sharding import PartitionSpec as P


def shards(tokens, cotangent, first_factor, second_factor, gate_source, alternate):
    inputs = tokens[0]
    rows_here = inputs.shape[0]
    width = inputs.shape[1]
    order_len = alternate.shape[0]
    blocks_here = rows_here // order_len
    select = (lax.broadcasted_iota(jnp.int32, (width, width), 0) == gate_source[None, :]).astype(
        jnp.bfloat16
    )
    gate = jax.nn.sigmoid(jnp.dot(inputs, select, preferred_element_type=jnp.float32))
    first_full = lax.all_gather(first_factor, "batch", axis=1, tiled=True)
    second_full = lax.all_gather(second_factor, "batch", axis=1, tiled=True)
    blocked = inputs.reshape(blocks_here, order_len, width)
    mixed = jnp.einsum(
        "ikj,ijc->ikc", first_full, blocked, preferred_element_type=jnp.float32
    ).astype(jnp.bfloat16)
    shuffled = jnp.take(mixed, alternate, axis=1)
    piece = lax.all_to_all(shuffled, "seq", split_axis=1, concat_axis=0, tiled=True)
    z_blocks = jnp.einsum("jmi,ijc->jmc", second_full, piece, preferred_element_type=jnp.float32)
    j_here = z_blocks.shape[0]
    count_second = z_blocks.shape[1]
    z_out = z_blocks.reshape(rows_here, width)
    cot = cotangent[0].astype(jnp.float32)
    dz_out = (cot * gate).astype(jnp.bfloat16)
    dgate = cot * z_out * gate * (1.0 - gate)
    dz_blocks = dz_out.reshape(j_here, count_second, width)
    term_second = jnp.einsum("jmc,ijc->jmi", dz_blocks, piece, preferred_element_type=jnp.float32)
    second_back = lax.all_gather(second_factor, "batch", axis=1, tiled=True)
    first_back = lax.all_gather(first_factor, "batch", axis=1, tiled=True)
    grad_two = lax.psum_scatter(
        term_second.astype(jnp.bfloat16), "batch", scatter_dimension=1, tiled=True
    )
    dregrouped = jnp.einsum(
        "jmi,jmc->ijc", second_back, dz_blocks, preferred_element_type=jnp.float32
    ).astype(jnp.bfloat16)
    positions = lax.iota(jnp.int32, order_len)
    inverse = jnp.zeros((order_len,), jnp.int32).at[alternate].set(positions)
    restored = jnp.take(
        lax.all_to_all(dregrouped, "seq", split_axis=0, concat_axis=1, tiled=True), inverse, axis=1
    )
    dmix_in = jnp.einsum("ikj,ikc->ijc", first_back, restored, preferred_element_type=jnp.float32)
    term_first = jnp.einsum("ikc,ijc->ikj", restored, blocked, preferred_element_type=jnp.float32)
    grad_one = lax.psum_scatter(
        term_first.astype(jnp.bfloat16), "batch", scatter_dimension=1, tiled=True
    )
    spread = jnp.dot(dgate, select.T.astype(jnp.float32), precision=lax.Precision.HIGHEST)
    grad_tokens = (dmix_in.reshape(rows_here, width) + spread).astype(jnp.bfloat16)
    return (grad_tokens[None], grad_one, grad_two)


def solution(mesh):
    in_specs = (
        P("batch", "seq", None),
        P("batch", "seq", None),
        P("seq", "batch", None),
        P("seq", "batch", None),
        P(),
        P(),
    )
    out_specs = (P("batch", "seq", None), P("seq", "batch", None), P("seq", "batch", None))
    return jax.shard_map(shards, mesh=mesh, in_specs=in_specs, out_specs=out_specs, check_vma=False)
```

profile of v0, /device:TPU:1, one launch (start us, length us, event | category | flops | bytes accessed | tf_op | source)
XLA Modules:
  0.0 260.4 jit_solution(14083302831994994531)
XLA Ops:
  7.2 0.7 all-gather.5.cloned.1.call-update
  7.9 0.7 compare_select_fusion.1
  8.6 0.7 compare_and_fusion
  9.3 40.9 %all-gather.5.cloned.1.call-done = bf16[4,512,512]{2,1,0:T(8,128)(2,1)} async-done(((bf16[4,128,512]{2,1,0:T(8,128)(2,1)}), bf16[4,512,512]{2,1,0:T(8,128)(2,1)}) %all-gather.5.cloned.1.call-update) | async-done | bytes 2097168 | tf_op jit(solution)/shard_map/all_gather | solution.py:35
  50.2 2.3 convolution_convert_fusion.2
  52.5 0.8 copy.35
  53.3 2.4 gather_fusion.1
  55.7 2.6 %select_bitcast_fusion = bf16[4,512,256]{2,0,1:T(4,128)(2,1)} fusion(bf16[512,4,256]{2,1,0:T(4,128)(2,1)S(1)} %gather_fusion.1, pred[512]{0:T(512)(128)(4,1)S(1)} %compare_and_fusion), kind=kLoop, calls=%fused_computation.26 | loop fusion | flops 524288 | bytes 2097664 | tf_op jit(solution)/shard_map/jit(_take)/select_n | solution.py:23
  58.3 17.3 %all-to-all-start.1 = ((bf16[4,512,256]{2,0,1:T(4,128)(2,1)}), bf16[4,512,256]{2,0,1:T(4,128)(2,1)}, u32[]{:S(2)}, u32[]{:S(2)}) async-start(bf16[4,512,256]{2,0,1:T(4,128)(2,1)} %select_bitcast_fusion), calls=%async_computation.1 | async-start | bytes 2097152 | tf_op jit(solution)/shard_map/all_to_all | solution.py:24
  75.7 0.7 all-gather.3.cloned.1.call-update
  77.0 2.5 fusion.6
  79.5 1.5 copy.42
  81.0 35.6 %all-gather.3.cloned.1.call-done = bf16[4,512,512]{2,1,0:T(8,128)(2,1)} async-done(((bf16[4,128,512]{2,1,0:T(8,128)(2,1)}), bf16[4,512,512]{2,1,0:T(8,128)(2,1)}) %all-gather.3.cloned.1.call-update) | async-done | bytes 2097168 | tf_op jit(solution)/shard_map/all_gather | solution.py:34
  116.6 2.3 fusion.11
  119.0 1.4 copy.31
  120.4 8.0 %all-to-all-done.1 = bf16[4,512,256]{2,0,1:T(4,128)(2,1)} async-done(((bf16[4,512,256]{2,0,1:T(4,128)(2,1)}), bf16[4,512,256]{2,0,1:T(4,128)(2,1)}, u32[]{:S(2)}, u32[]{:S(2)}) %all-to-all-start.1) | async-done | bytes 1048608 | tf_op jit(solution)/shard_map/all_to_all | solution.py:24
  128.4 9.9 %all-to-all-start = ((bf16[512,4,256]{2,1,0:T(4,128)(2,1)}), bf16[512,4,256]{2,1,0:T(4,128)(2,1)}, u32[]{:S(2)}, u32[]{:S(2)}) async-start(bf16[512,4,256]{2,1,0:T(4,128)(2,1)} %copy.31), calls=%async_computation | async-start | bytes 2097152 | tf_op jit(solution)/shard_map/all_to_all | solution.py:45
  138.3 1.6 copy.36
  140.0 2.1 convolution_convert_fusion
  142.1 2.6 %scatter_custom_fusion = s32[512]{0:T(512)S(1)} fusion(s32[512]{0:T(512)S(1)} %compare_select_fusion.1, s32[512]{0:T(512)S(1)} %iota.9, s32[]{:T(128)} %constant.3.clone.1), kind=kCustom, calls=%fused_computation.43 | custom fusion | bytes 2052 | tf_op jit(solution)/shard_map/scatter | solution.py:43
  144.8 45.4 %all-to-all-done = bf16[512,4,256]{2,1,0:T(4,128)(2,1)} async-done(((bf16[512,4,256]{2,1,0:T(4,128)(2,1)}), bf16[512,4,256]{2,1,0:T(4,128)(2,1)}, u32[]{:S(2)}, u32[]{:S(2)}) %all-to-all-start) | async-done | bytes 1048608 | tf_op jit(solution)/shard_map/all_to_all | solution.py:45
  190.2 1.6 copy.32
  191.8 2.9 %gather_fusion = bf16[512,4,256]{2,1,0:T(4,128)(2,1)} fusion(bf16[4,512,256]{2,0,1:T(4,128)(2,1)S(1)} %bitcast.56, s32[1024]{0:T(1024)S(1)} %pad_clamp_fusion.1), kind=kCustom, calls=%fused_computation.clone | custom fusion | bytes 2099200 | tf_op jit(solution)/shard_map/jit(_take)/gather | solution.py:44
  194.8 3.1 %select_bitcast_fusion.1 = bf16[4,512,256]{2,0,1:T(4,128)(2,1)S(1)} fusion(bf16[512,4,256]{2,1,0:T(4,128)(2,1)} %gather_fusion, pred[512]{0:T(512)(128)(4,1)S(1)} %compare_and_fusion.1), kind=kLoop, calls=%fused_computation.27 | loop fusion | flops 524288 | bytes 2097664 | tf_op jit(solution)/shard_map/jit(_take)/select_n | solution.py:44
  197.9 2.1 convolution_convert_fusion.1
  200.0 2.4 convolution_bitcast_fusion
  202.4 1.5 copy.43
  204.0 0.8 copy-done.3
  204.8 2.1 convolution_bitcast_fusion.1
  206.9 3.1 %copy.34 = f32[4,512,256]{2,1,0:T(8,128)} copy(f32[4,512,256]{1,2,0:T(8,128)} %convolution_bitcast_fusion.1) | data formatting | bytes 4194304 | tf_op jit(solution)/shard_map/ikj,ikc->ijc/dot_general | solution.py:47
  209.9 5.4 %fusion.5 = bf16[1,2048,256]{2,1,0:T(8,128)(2,1)} fusion(f32[2048,256]{1,0:T(8,128)} %bitcast.55, f32[2048,256]{0,1:T(8,128)} %get-tuple-element.5, f32[2048,256]{0,1:T(8,128)S(1)} %bitcast.54, bf16[1,2048,256]{1,2,0:T(8,128)(2,1)} %copy-done.2, s32[256]{0:T(256)S(1)} %copy-done.5), kind=kOutput, calls=%fused_computation.12 | convolution fusion | flops 1614348288 | bytes 8389632 | tf_op jit(solution)/shard_map/dot_general | solution.py:52
  215.4 38.5 %reduce-scatter.3.cloned.1.call-done = bf16[4,128,512]{2,1,0:T(8,128)(2,1)} async-done(((bf16[4,512,512]{2,1,0:T(8,128)(2,1)}), bf16[4,128,512]{2,1,0:T(8,128)(2,1)}) %reduce-scatter.3.cloned.1.call-update) | async-done | bytes 524304 | tf_op jit(solution)/shard_map/reduce_scatter | solution.py:49
  (24 shorter events, 0.9 us)
Async XLA Ops:
  7.2 43.0 %copy-start = (bf16[1,2048,256]{2,1,0:T(8,128)(2,1)S(1)}, bf16[1,2048,256]{2,1,0:T(8,128)(2,1)}, u32[]{:S(2)}) copy-start(bf16[1,2048,256]{2,1,0:T(8,128)(2,1)} %param.8) | copy-start | bytes 3145732
  7.2 43.0 %all-gather.5.cloned.1.call-start = ((), (), s32[]{:S(2)}) async-start(), calls=%async_computation.5 | async-start | bytes 2621440 | tf_op jit(solution)/shard_map/all_gather | solution.py:35
  55.7 20.7 %copy-start.4 = (bf16[1,2048,256]{2,1,0:T(8,128)(2,1)S(1)}, bf16[1,2048,256]{2,1,0:T(8,128)(2,1)}, u32[]{:S(2)}) copy-start(bf16[1,2048,256]{2,1,0:T(8,128)(2,1)} %param.9) | copy-start | bytes 3145732
  58.3 18.7 %copy-start.5 = (s32[256]{0:T(256)S(1)}, s32[256]{0:T(256)}, u32[]{:S(2)}) copy-start(s32[256]{0:T(256)} %param.12) | copy-start | bytes 3076
  58.3 70.1 %all-to-all-start.1 = ((bf16[4,512,256]{2,0,1:T(4,128)(2,1)}), bf16[4,512,256]{2,0,1:T(4,128)(2,1)}, u32[]{:S(2)}, u32[]{:S(2)}) async-start(bf16[4,512,256]{2,0,1:T(4,128)(2,1)} %select_bitcast_fusion), calls=%async_computation.1 | async-start | bytes 2097152 | tf_op jit(solution)/shard_map/all_to_all | solution.py:24
  75.6 41.0 %all-gather.3.cloned.1.call-start = ((), (), s32[]{:S(2)}) async-start(), calls=%async_computation.4 | async-start | bytes 2621440 | tf_op jit(solution)/shard_map/all_gather | solution.py:34
  77.0 2.5 copy-start.2
  128.4 61.8 %all-to-all-start = ((bf16[512,4,256]{2,1,0:T(4,128)(2,1)}), bf16[512,4,256]{2,1,0:T(4,128)(2,1)}, u32[]{:S(2)}, u32[]{:S(2)}) async-start(bf16[512,4,256]{2,1,0:T(4,128)(2,1)} %copy.31), calls=%async_computation | async-start | bytes 2097152 | tf_op jit(solution)/shard_map/all_to_all | solution.py:45
  138.3 77.1 %reduce-scatter.5.cloned.1.call-start = ((), (), s32[]{:S(2)}) async-start(), calls=%async_computation.7 | async-start | bytes 2621440 | tf_op jit(solution)/shard_map/reduce_scatter | solution.py:36
  142.1 111.8 %reduce-scatter.3.cloned.1.call-start = ((), (), s32[]{:S(2)}) async-start(), calls=%async_computation.6 | async-start | bytes 2621440 | tf_op jit(solution)/shard_map/reduce_scatter | solution.py:49
  202.4 2.3 copy-start.3
  206.9 3.1 %copy-start.1 = (f32[4,32,8,512]{3,2,0,1:T(8,128)S(1)}, f32[4,32,8,512]{3,2,0,1:T(8,128)}, u32[]{:S(2)}) copy-start(f32[4,32,8,512]{3,2,0,1:T(8,128)} %copy.43) | copy-start | bytes 6291460
Sparse Core Ops, SparseCore 0:
  10.1 39.9 all-gather.4
  78.6 38.0 all-gather.2
  142.7 54.3 reduce-scatter.4
  201.0 52.8 reduce-scatter.2
where the time goes:
time: 261 us; the launch traced here: 260 us
  waiting for transfers between devices  170 us (65%)
  starting transfers between devices  27.3 us (10%)
  matrix products  21.2 us (8%)
  local copies, waits for them, and re-layouts  21 us (8%)
  between operations  13.9 us (5%)
  other arithmetic  7.19 us (3%)
    all_to_all x1, waiting for transfers between devices, shards(): lax.all_to_all(dregrouped, 'seq', split_axis=0, concat_axis=1, tiled=True)  45.4 us
    all_gather x1, waiting for transfers between devices, shards(): first_back = lax.all_gather(first_factor, 'batch', axis=1, tiled=True)  40.9 us
    reduce_scatter x1, waiting for transfers between devices, shards(): lax.psum_scatter(term_first.astype(jnp.bfloat16), 'batch', scatter_dimens...  38.5 us
    all_gather x1, waiting for transfers between devices, shards(): second_back = lax.all_gather(second_factor, 'batch', axis=1, tiled=True)  35.6 us
    all_to_all x1, starting transfers between devices, shards(): lax.all_to_all(shuffled, 'seq', split_axis=1, concat_axis=0, tiled=True)  17.3 us
    all_to_all x1, starting transfers between devices, shards(): lax.all_to_all(dregrouped, 'seq', split_axis=0, concat_axis=1, tiled=True)  9.85 us
    all_to_all x1, waiting for transfers between devices, shards(): lax.all_to_all(shuffled, 'seq', split_axis=1, concat_axis=0, tiled=True)  8.01 us
    dot_general x1, matrix products, shards(): jnp.dot(dgate, select.T.astype(jnp.float32), precision=lax.Precision.HIGH...  5.45 us
  transfers between devices with their start and end apart: 6, of which 5 were waited for; matrix products, arithmetic and copies ran while one was open for 16% of the time, Pallas kernels for 0%

commit v1 on v0

v1 whole, which is shorter than its diff:
```python
import functools

import jax
import jax.numpy as jnp
from jax import lax
from jax.experimental import pallas as pl
from jax.experimental.pallas import tpu as pltpu
from jax.sharding import PartitionSpec as P

MESH = pl.DeviceIdType.MESH
BF = jnp.bfloat16
F32 = jnp.float32


def push(src, dst, send_sem, recv_sem, device):
    return pltpu.make_async_remote_copy(
        src_ref=src,
        dst_ref=dst,
        send_sem=send_sem,
        recv_sem=recv_sem,
        device_id=device,
        device_id_type=MESH,
    )


def dot(a, b, da=1, db=0):
    return lax.dot_general(a, b, (((da,), (db,)), ((), ())), preferred_element_type=F32)


def kernel(
    n,
    tokens,
    cot,
    first,
    second,
    source,
    alt,
    grad_tokens,
    grad_first,
    grad_second,
    full,
    select,
    gate,
    dz,
    spread,
    pick,
    pick_t,
    mix4,
    mix8,
    column,
    send1,
    land1,
    send2,
    land2,
    regrouped,
    dcolumn,
    dmixed,
    term,
    near,
    staged,
    away,
    ag_send,
    ag_recv,
    a2a_send,
    a2a_recv,
    rs_send,
    rs_recv,
):
    order = alt.shape[1]
    width = tokens.shape[1]
    nb = first.shape[0]
    part = first.shape[1]
    group = min(16, n)
    groups = n // group
    span = group * nb
    s = lax.axis_index("seq")
    b = lax.axis_index("batch")
    other = b + 1 - 2 * lax.rem(b, 2)
    far = lax.rem(b + 2, 4)
    other_far = lax.rem(other + 2, 4)
    shards = (first, second)

    barrier = pltpu.get_barrier_semaphore()
    for peer in (other, far):
        pl.semaphore_signal(barrier, inc=1, device_id={"batch": peer}, device_id_type=MESH)

    def greet(r, carry):
        pl.semaphore_signal(
            barrier, inc=1, device_id={"seq": lax.rem(s + r, n)}, device_id_type=MESH
        )
        return carry

    lax.fori_loop(1, n, greet, 0)

    row = lax.broadcasted_iota(jnp.int32, (order, order), 0)
    hit = (row == alt[...]).astype(F32)
    pick_t[...] = hit.astype(BF)
    pick[...] = hit.T.astype(BF)
    select[...] = (
        lax.broadcasted_iota(jnp.int32, (width, width), 0) == source[...]
    ).astype(F32).astype(BF)
    rows4 = group * 8
    r4 = lax.broadcasted_iota(jnp.int32, (rows4, rows4), 0)
    c4 = lax.broadcasted_iota(jnp.int32, (rows4, rows4), 1)
    want = ((r4 // 4) % 2) * span + (r4 // 8) * 4 + r4 % 4
    mix4[...] = (want == c4).astype(F32).astype(BF)
    rows8 = group * 16
    r8 = lax.broadcasted_iota(jnp.int32, (rows8, rows8), 0)
    c8 = lax.broadcasted_iota(jnp.int32, (rows8, rows8), 1)
    want = (r8 % 4) * span + ((r8 // 8) % group) * 4 + (r8 // rows4) * 2 + (r8 // 4) % 2
    mix8[...] = (want == c8).astype(F32).astype(BF)
    for f in range(2):
        full[f, :, b] = shards[f][...]

    pl.semaphore_wait(barrier, n + 1)

    def to_far(f, i):
        return push(
            shards[f].at[i], full.at[f, i, b], ag_send.at[f, i, 0], ag_recv.at[f, i, 0], {"batch": far}
        )

    def to_other(f, i):
        return push(
            shards[f].at[i], full.at[f, i, b], ag_send.at[f, i, 1], ag_recv.at[f, i, 1], {"batch": other}
        )

    def onward(f, i):
        return push(
            full.at[f, i, far], full.at[f, i, far], ag_send.at[f, i, 2], ag_recv.at[f, i, 2], {"batch": other}
        )

    for f in range(2):
        for i in range(nb):
            to_far(f, i).start()
            to_other(f, i).start()

    def block(f, i):
        return full[f, i].reshape(order, order)

    def exchange(k, h, buf, land):
        def go(r, carry):
            p = lax.rem(s + r, n)
            push(
                buf.at[h, p], land.at[h, s], a2a_send.at[k, h], a2a_recv.at[k, h], {"seq": p}
            ).start()
            return carry

        lax.fori_loop(1, n, go, 0)
        land[h, s] = buf[h, s]

    def exchanged(k, h, buf, land):
        rest = pl.ds(0, n - 1)
        return push(
            buf.at[h, rest],
            land.at[h, rest],
            a2a_send.at[k, h],
            a2a_recv.at[k, h],
            {"seq": lax.rem(s + 1, n)},
        )

    for h in range(2):
        for i in (2 * h, 2 * h + 1):
            to_far(0, i).wait_recv()
            onward(0, i).start()
        for i in (2 * h, 2 * h + 1):
            to_other(0, i).wait_recv()
            onward(0, i).wait_recv()

            def apply(i2, carry, h=h):
                i = 2 * h + i2
                x = tokens[pl.ds(pl.multiple_of(i * order, order), order), :]
                mixed = dot(block(0, i), x).astype(BF)
                regrouped[i2] = dot(pick[...], mixed).astype(BF)
                return carry

            apply(i - 2 * h, 0)

        def pack(g, carry, h=h):
            at = pl.ds(pl.multiple_of(g * span, span), span)
            stack = jnp.concatenate([regrouped[0, at], regrouped[1, at]], axis=0)
            out = dot(mix4[...], stack)
            send1[h, pl.ds(g * group, group)] = out.reshape(group, 8, width).astype(BF)
            return carry

        lax.fori_loop(0, groups, pack, 0)
        exchange(0, h, send1, land1)

    def gating(q, carry):
        at = pl.ds(pl.multiple_of(q * order, order), order)
        g = jax.nn.sigmoid(dot(tokens[at, :], select[...]))
        gate[at, :] = g
        dz[at, :] = (cot[at, :].astype(F32) * g).astype(BF)
        return carry

    for i in range(nb):
        to_far(1, i).wait_recv()
        onward(1, i).start()
    lax.fori_loop(0, nb, gating, 0)
    for i in range(nb):
        to_other(1, i).wait_recv()
        onward(1, i).wait_recv()

    def back(j, carry):
        at = pl.ds(pl.multiple_of(j * order, order), order)
        dcolumn[j] = dot(block(1, j), dz[at, :], 0, 0).astype(BF)
        return carry

    lax.fori_loop(0, nb, back, 0)

    def pack_back(g, carry):
        at = pl.ds(pl.multiple_of(g * span, span), span)
        stack = jnp.concatenate([dcolumn[j, at] for j in range(nb)], axis=0)
        out = dot(mix8[...], stack)
        where = pl.ds(g * group, group)
        send2[0, where] = out[:rows4].reshape(group, 8, width).astype(BF)
        send2[1, where] = out[rows4:].reshape(group, 8, width).astype(BF)
        return carry

    lax.fori_loop(0, groups, pack_back, 0)
    for h in range(2):
        exchange(1, h, send2, land2)

    def near_own(f, q):
        return push(
            term.at[f, q, other], near.at[f, q, 0], rs_send.at[f, q, 0], rs_recv.at[f, q, 0], {"batch": other}
        )

    def near_far(f, q):
        return push(
            term.at[f, q, other_far], near.at[f, q, 1], rs_send.at[f, q, 1], rs_recv.at[f, q, 1], {"batch": other}
        )

    def across(f, q):
        return push(
            staged.at[f, q], away.at[f, q], rs_send.at[f, q, 2], rs_recv.at[f, q, 2], {"batch": far}
        )

    def middle(f, q):
        near_own(f, q).wait_recv()
        near_far(f, q).wait_recv()
        staged[f, q] = (term[f, q, far].astype(F32) + near[f, q, 1].astype(F32)).astype(BF)
        across(f, q).start()

    def finish(f, q, out):
        across(f, q).wait_recv()
        here = term[f, q, b].astype(F32) + near[f, q, 0].astype(F32)
        out[q] = (here + away[f, q].astype(F32)).astype(BF)

    for h in range(2):
        exchanged(0, h, send1, land1).wait_recv()

    def unpack(g, carry):
        where = pl.ds(g * group, group)
        halves = [land1[h, where].astype(F32).reshape(rows4, width).astype(BF) for h in range(2)]
        out = dot(mix8[...], jnp.concatenate(halves, axis=0), 0, 0).astype(BF)
        at = pl.ds(pl.multiple_of(g * span, span), span)
        for j in range(nb):
            column[j, at] = out[j * span : (j + 1) * span]
        return carry

    lax.fori_loop(0, groups, unpack, 0)

    def ahead(j, carry):
        at = pl.ds(pl.multiple_of(j * order, order), order)
        here = column[j]
        term[1, j] = dot(dz[at, :], here, 1, 1).astype(BF).reshape(4, part, order)
        near_own(1, j).start()
        near_far(1, j).start()
        z = dot(block(1, j), here)
        g = gate[at, :]
        dgate = cot[at, :].astype(F32) * z * g * (1.0 - g)
        high = dgate.astype(BF)
        low = (dgate - high.astype(F32)).astype(BF)
        spread[at, :] = dot(high, select[...], 1, 1) + dot(low, select[...], 1, 1)
        return carry

    lax.fori_loop(0, nb, ahead, 0)
    for q in range(nb):
        middle(1, q)
    for q in range(nb):
        finish(1, q, grad_second)

    for h in range(2):
        exchanged(1, h, send2, land2).wait_recv()

        def unpack_back(g, carry, h=h):
            piece = land2[h, pl.ds(g * group, group)].astype(F32).reshape(rows4, width).astype(BF)
            out = dot(mix4[...], piece, 0, 0).astype(BF)
            at = pl.ds(pl.multiple_of(g * span, span), span)
            regrouped[0, at] = out[:span]
            regrouped[1, at] = out[span:]
            return carry

        lax.fori_loop(0, groups, unpack_back, 0)

        def under(i2, carry, h=h):
            i = 2 * h + i2
            at = pl.ds(pl.multiple_of(i * order, order), order)
            dm = dot(pick_t[...], regrouped[i2]).astype(BF)
            dmixed[i2] = dm
            term[0, i] = dot(dm, tokens[at, :], 1, 1).astype(BF).reshape(4, part, order)
            near_own(0, i).start()
            near_far(0, i).start()
            return carry

        lax.fori_loop(0, 2, under, 0)

        def down(i2, carry, h=h):
            i = 2 * h + i2
            at = pl.ds(pl.multiple_of(i * order, order), order)
            inner = dot(block(0, i), dmixed[i2], 0, 0)
            grad_tokens[at, :] = (inner + spread[at, :]).astype(BF)
            middle(0, i)
            return carry

        lax.fori_loop(0, 2, down, 0)
    for q in range(nb):
        finish(0, q, grad_first)

    for f in range(2):
        for i in range(nb):
            to_far(f, i).wait_send()
            to_other(f, i).wait_send()
            onward(f, i).wait_send()
            near_own(f, i).wait_send()
            near_far(f, i).wait_send()
            across(f, i).wait_send()
    for h in range(2):
        exchanged(0, h, send1, land1).wait_send()
        exchanged(1, h, send2, land2).wait_send()


def solution(mesh):
    n = mesh.shape["seq"]

    def shards(tokens, cotangent, first_factor, second_factor, gate_source, alternate):
        nb, part, order = first_factor.shape
        rows, width = tokens.shape[1:]
        group = min(16, n)
        vmem = pltpu.VMEM
        out = pl.pallas_call(
            functools.partial(kernel, n),
            out_shape=[
                jax.ShapeDtypeStruct((rows, width), BF),
                jax.ShapeDtypeStruct((nb, part, order), BF),
                jax.ShapeDtypeStruct((nb, part, order), BF),
            ],
            in_specs=[pl.BlockSpec(memory_space=vmem)] * 6,
            out_specs=[pl.BlockSpec(memory_space=vmem)] * 3,
            scratch_shapes=[
                vmem((2, nb, 4, part, order), BF),
                vmem((width, width), BF),
                vmem((rows, width), F32),
                vmem((rows, width), BF),
                vmem((rows, width), F32),
                vmem((order, order), BF),
                vmem((order, order), BF),
                vmem((group * 8, group * 8), BF),
                vmem((group * 16, group * 16), BF),
                vmem((nb, order, width), BF),
                vmem((2, n, 8, width), BF),
                vmem((2, n, 8, width), BF),
                vmem((2, n, 8, width), BF),
                vmem((2, n, 8, width), BF),
                vmem((2, order, width), BF),
                vmem((nb, order, width), BF),
                vmem((2, order, width), BF),
                vmem((2, nb, 4, part, order), BF),
                vmem((2, nb, 2, part, order), BF),
                vmem((2, nb, part, order), BF),
                vmem((2, nb, part, order), BF),
                pltpu.SemaphoreType.DMA((2, nb, 3)),
                pltpu.SemaphoreType.DMA((2, nb, 3)),
                pltpu.SemaphoreType.DMA((2, 2)),
                pltpu.SemaphoreType.DMA((2, 2)),
                pltpu.SemaphoreType.DMA((2, nb, 3)),
                pltpu.SemaphoreType.DMA((2, nb, 3)),
            ],
            compiler_params=pltpu.CompilerParams(
                collective_id=0, has_side_effects=True, vmem_limit_bytes=56 << 20
            ),
        )(
            tokens[0],
            cotangent[0],
            first_factor,
            second_factor,
            gate_source.reshape(1, -1),
            alternate.reshape(1, -1),
        )
        return out[0][None], out[1], out[2]

    in_specs = (
        P("batch", "seq", None),
        P("batch", "seq", None),
        P("seq", "batch", None),
        P("seq", "batch", None),
        P(),
        P(),
    )
    out_specs = (P("batch", "seq", None), P("seq", "batch", None), P("seq", "batch", None))
    return jax.shard_map(shards, mesh=mesh, in_specs=in_specs, out_specs=out_specs, check_vma=False)
```

time: 261 us -> 146 us (0.56)
  waiting for transfers between devices: 170 us -> 0 us
  Pallas kernels: 0 us -> 141 us
  starting transfers between devices: 27.3 us -> 0 us
  matrix products: 21.2 us -> 0 us
  local copies, waits for them, and re-layouts: 21 us -> 4.35 us
  between operations: 13.9 us -> 0.65 us
  other arithmetic: 7.19 us -> 0 us
    pallas_call x0 -> x1, Pallas kernels: none -> 141 us  [shards(): pl.pallas_call(functools.partial(kernel, n), out_shape=[jax.ShapeDtypeStr...]
    all_gather x2 -> x0, waiting for transfers between devices: 76.5 us -> none  [the longest x1 40.9 us: shards(): first_back = lax.all_gather(first_factor, 'batch', axis=1, tiled=True)]
    all_to_all x2 -> x0, waiting for transfers between devices: 53.4 us -> none  [the longest x1 45.4 us: shards(): lax.all_to_all(dregrouped, 'seq', split_axis=0, concat_axis=1, tiled=True)]
    reduce_scatter x2 -> x0, waiting for transfers between devices: 38.5 us -> none  [the longest x1 38.5 us: shards(): lax.psum_scatter(term_first.astype(jnp.bfloat16), 'batch', scatter_dimens...]
    all_to_all x2 -> x0, starting transfers between devices: 27.1 us -> none  [the longest x1 17.3 us: shards(): lax.all_to_all(shuffled, 'seq', split_axis=1, concat_axis=0, tiled=True)]
    dot_general x8 -> x0, matrix products: 21.2 us -> none  [the longest x1 5.45 us: shards(): jnp.dot(dgate, select.T.astype(jnp.float32), precision=lax.Precision.HIGH...]
    select_n x4 -> x0, other arithmetic: 6.48 us -> none  [the longest x2 3.15 us: shards(): jnp.take(lax.all_to_all(dregrouped, 'seq', split_axis=0, concat_axis=1, t...]
    gather x2 -> x0, local copies, waits for them, and re-layouts: 5.34 us -> none  [the longest x1 2.95 us: shards(): jnp.take(lax.all_to_all(dregrouped, 'seq', split_axis=0, concat_axis=1, t...]
  transfers between devices with their start and end apart: 6 -> 0, of which waited for: 5 -> 0; matrix products, arithmetic and copies ran while one was open for 16% -> 0% of each run, Pallas kernels for 0% -> 0%
where the time goes in v1:
time: 146 us
  Pallas kernels  141 us (97%)
  local copies, waits for them, and re-layouts  4.35 us (3%)
    pallas_call x1, Pallas kernels, shards(): pl.pallas_call(functools.partial(kernel, n), out_shape=[jax.ShapeDtypeStr...  141 us
    unnamed x7, local copies, waits for them, and re-layouts  4.35 us

profile of v1, /device:TPU:1, one launch (start us, length us, event | category | flops | bytes accessed | tf_op | source)
XLA Modules:
  0.0 146.0 jit_solution(9691204932122795644)
XLA Ops:
  0.6 141.0 %shard_map.85 = (bf16[2048,256]{1,0:T(8,128)(2,1)}, bf16[4,128,512]{2,1,0:T(8,128)(2,1)}, bf16[4,128,512]{2,1,0:T(8,128)(2,1)}) custom-call(bf16[2048,256]{1,0:T(8,128)(2,1)} %bitcast.5, bf16[2048,256]{1,0:T(8,128)(2,1)} %bitcast.6, bf16[4,128,512]{2,1,0:T(8,128)(2,1)} %first.1, bf16[4,128,512]{2,1,0:T(8,128)(2,1)} %second.1, s32[1,256]{1,0:T(1,128)} %bitcast.9, ...), custom_call_target="tpu_custom_call" | custom-call | tf_op jit(solution)/shard_map/pallas_call | solution.py:341
  141.7 0.0 copy-start.1
  141.7 2.3 %copy.12 = bf16[1,2048,256]{2,1,0:T(8,128)(2,1)} copy(bf16[1,2048,256]{2,1,0:T(8,128)(2,1)} %bitcast.7) | data formatting | bytes 2097152
  144.0 0.0 copy-done.1
  144.0 0.0 copy-start
  144.0 0.8 copy.13
  144.8 0.4 copy-done
  145.2 0.8 copy.14
Async XLA Ops:
  141.7 2.3 %copy-start.1 = (bf16[4,128,512]{2,1,0:T(8,128)(2,1)S(1)}, bf16[4,128,512]{2,1,0:T(8,128)(2,1)}, u32[]{:S(2)}) copy-start(bf16[4,128,512]{2,1,0:T(8,128)(2,1)} %get-tuple-element.13) | copy-start | bytes 1572868
  144.0 1.2 copy-start

commit v2 on v1

--- a/solution.py
+++ b/solution.py
@@ -29,8 +29,8 @@
 
 def kernel(
     n,
-    tokens,
-    cot,
+    tokens_in,
+    cot_in,
     first,
     second,
     source,
@@ -38,6 +38,8 @@
     grad_tokens,
     grad_first,
     grad_second,
+    tokens,
+    cot,
     full,
     select,
     gate,
@@ -47,11 +49,16 @@
     pick_t,
     mix4,
     mix8,
+    mixq,
     column,
     send1,
     land1,
+    send1q,
+    land1q,
     send2,
     land2,
+    send2q,
+    land2q,
     regrouped,
     dcolumn,
     dmixed,
@@ -65,6 +72,7 @@
     a2a_recv,
     rs_send,
     rs_recv,
+    in_sem,
 ):
     order = alt.shape[1]
     width = tokens.shape[1]
@@ -91,6 +99,35 @@
         return carry
 
     lax.fori_loop(1, n, greet, 0)
+
+    loads = [pltpu.make_async_copy(tokens_in, tokens, in_sem.at[0])]
+    for f in range(2):
+        loads.append(pltpu.make_async_copy(shards[f], full.at[f, :, b], in_sem.at[1 + f]))
+    loads.append(pltpu.make_async_copy(cot_in, cot, in_sem.at[3]))
+    for load in loads:
+        load.start()
+
+    pl.semaphore_wait(barrier, n + 1)
+
+    def to_far(f, i):
+        return push(
+            shards[f].at[i], full.at[f, i, b], ag_send.at[f, i, 0], ag_recv.at[f, i, 0], {"batch": far}
+        )
+
+    def to_other(f, i):
+        return push(
+            shards[f].at[i], full.at[f, i, b], ag_send.at[f, i, 1], ag_recv.at[f, i, 1], {"batch": other}
+        )
+
+    def onward(f, i):
+        return push(
+            full.at[f, i, far], full.at[f, i, far], ag_send.at[f, i, 2], ag_recv.at[f, i, 2], {"batch": other}
+        )
+
+    for f in range(2):
+        for i in range(nb):
+            to_far(f, i).start()
+            to_other(f, i).start()
 
     row = lax.broadcasted_iota(jnp.int32, (order, order), 0)
     hit = (row == alt[...]).astype(F32)
@@ -109,81 +146,71 @@
     c8 = lax.broadcasted_iota(jnp.int32, (rows8, rows8), 1)
     want = (r8 % 4) * span + ((r8 // 8) % group) * 4 + (r8 // rows4) * 2 + (r8 // 4) % 2
     mix8[...] = (want == c8).astype(F32).astype(BF)
-    for f in range(2):
-        full[f, :, b] = shards[f][...]
-
-    pl.semaphore_wait(barrier, n + 1)
-
-    def to_far(f, i):
-        return push(
-            shards[f].at[i], full.at[f, i, b], ag_send.at[f, i, 0], ag_recv.at[f, i, 0], {"batch": far}
-        )
-
-    def to_other(f, i):
-        return push(
-            shards[f].at[i], full.at[f, i, b], ag_send.at[f, i, 1], ag_recv.at[f, i, 1], {"batch": other}
-        )
-
-    def onward(f, i):
-        return push(
-            full.at[f, i, far], full.at[f, i, far], ag_send.at[f, i, 2], ag_recv.at[f, i, 2], {"batch": other}
-        )
-
-    for f in range(2):
-        for i in range(nb):
-            to_far(f, i).start()
-            to_other(f, i).start()
+    rq = lax.broadcasted_iota(jnp.int32, (rows8, 2 * rows8), 0)
+    cq = lax.broadcasted_iota(jnp.int32, (rows8, 2 * rows8), 1)
+    want = ((rq // 4) % 2) * rows8 + (rq % 4) * span + ((rq // 8) % group) * 4 + rq // rows4
+    for h in range(2):
+        mixq[h] = (want + 2 * h == cq).astype(F32).astype(BF)
+
+    loads[0].wait()
+    loads[1].wait()
 
     def block(f, i):
         return full[f, i].reshape(order, order)
 
-    def exchange(k, h, buf, land):
+    def exchange(k, buf, land):
         def go(r, carry):
             p = lax.rem(s + r, n)
-            push(
-                buf.at[h, p], land.at[h, s], a2a_send.at[k, h], a2a_recv.at[k, h], {"seq": p}
-            ).start()
+            push(buf.at[p], land.at[s], a2a_send.at[k], a2a_recv.at[k], {"seq": p}).start()
             return carry
 
         lax.fori_loop(1, n, go, 0)
-        land[h, s] = buf[h, s]
-
-    def exchanged(k, h, buf, land):
+        land[s] = buf[s]
+
+    def exchanged(k, buf, land):
         rest = pl.ds(0, n - 1)
         return push(
-            buf.at[h, rest],
-            land.at[h, rest],
-            a2a_send.at[k, h],
-            a2a_recv.at[k, h],
-            {"seq": lax.rem(s + 1, n)},
-        )
-
-    for h in range(2):
-        for i in (2 * h, 2 * h + 1):
-            to_far(0, i).wait_recv()
-            onward(0, i).start()
-        for i in (2 * h, 2 * h + 1):
-            to_other(0, i).wait_recv()
-            onward(0, i).wait_recv()
-
-            def apply(i2, carry, h=h):
-                i = 2 * h + i2
-                x = tokens[pl.ds(pl.multiple_of(i * order, order), order), :]
-                mixed = dot(block(0, i), x).astype(BF)
-                regrouped[i2] = dot(pick[...], mixed).astype(BF)
-                return carry
-
-            apply(i - 2 * h, 0)
-
-        def pack(g, carry, h=h):
+            buf.at[rest], land.at[rest], a2a_send.at[k], a2a_recv.at[k], {"seq": lax.rem(s + 1, n)}
+        )
+
+    lanes = width // 2
+
+    def apply(i, slot):
+        to_other(0, i).wait_recv()
+        onward(0, i).wait_recv()
+        mixed = dot(block(0, i), tokens[i * order : (i + 1) * order, :]).astype(BF)
+        regrouped[slot] = dot(pick[...], mixed).astype(BF)
+
+    for i in range(2):
+        to_far(0, i).wait_recv()
+        onward(0, i).start()
+        apply(i, i)
+
+        def pack_one(g, carry, i=i):
             at = pl.ds(pl.multiple_of(g * span, span), span)
-            stack = jnp.concatenate([regrouped[0, at], regrouped[1, at]], axis=0)
+            own = regrouped[i, at]
+            stack = jnp.concatenate([own[:, :lanes], own[:, lanes:]], axis=0)
             out = dot(mix4[...], stack)
-            send1[h, pl.ds(g * group, group)] = out.reshape(group, 8, width).astype(BF)
+            send1q[i, pl.ds(g * group, group)] = out.reshape(group, 8, lanes).astype(BF)
             return carry
 
-        lax.fori_loop(0, groups, pack, 0)
-        exchange(0, h, send1, land1)
+        lax.fori_loop(0, groups, pack_one, 0)
+        exchange(i, send1q.at[i], land1q.at[i])
+    for i in (2, 3):
+        to_far(0, i).wait_recv()
+        onward(0, i).start()
+    for i in (2, 3):
+        apply(i, i - 2)
+
+    def pack(g, carry):
+        at = pl.ds(pl.multiple_of(g * span, span), span)
+        stack = jnp.concatenate([regrouped[0, at], regrouped[1, at]], axis=0)
+        out = dot(mix4[...], stack)
+        send1[pl.ds(g * group, group)] = out.reshape(group, 8, width).astype(BF)
+        return carry
+
+    lax.fori_loop(0, groups, pack, 0)
+    exchange(2, send1, land1)
 
     def gating(q, carry):
         at = pl.ds(pl.multiple_of(q * order, order), order)
@@ -195,7 +222,9 @@
     for i in range(nb):
         to_far(1, i).wait_recv()
         onward(1, i).start()
+    loads[3].wait()
     lax.fori_loop(0, nb, gating, 0)
+    loads[2].wait()
     for i in range(nb):
         to_other(1, i).wait_recv()
         onward(1, i).wait_recv()
@@ -210,15 +239,19 @@
     def pack_back(g, carry):
         at = pl.ds(pl.multiple_of(g * span, span), span)
         stack = jnp.concatenate([dcolumn[j, at] for j in range(nb)], axis=0)
-        out = dot(mix8[...], stack)
         where = pl.ds(g * group, group)
-        send2[0, where] = out[:rows4].reshape(group, 8, width).astype(BF)
-        send2[1, where] = out[rows4:].reshape(group, 8, width).astype(BF)
+        out = dot(mix8[:rows4], stack)
+        send2[where] = out.reshape(group, 8, width).astype(BF)
+        halves = jnp.concatenate([stack[:, :lanes], stack[:, lanes:]], axis=0)
+        out = dot(mixq[1], halves)
+        send2q[0, where] = out[:rows4].reshape(group, 8, lanes).astype(BF)
+        send2q[1, where] = out[rows4:].reshape(group, 8, lanes).astype(BF)
         return carry
 
     lax.fori_loop(0, groups, pack_back, 0)
-    for h in range(2):
-        exchange(1, h, send2, land2)
+    exchange(3, send2, land2)
+    for q in range(2):
+        exchange(4 + q, send2q.at[q], land2q.at[q])
 
     def near_own(f, q):
         return push(
@@ -246,13 +279,17 @@
         here = term[f, q, b].astype(F32) + near[f, q, 0].astype(F32)
         out[q] = (here + away[f, q].astype(F32)).astype(BF)
 
-    for h in range(2):
-        exchanged(0, h, send1, land1).wait_recv()
+    for q in range(2):
+        exchanged(q, send1q.at[q], land1q.at[q]).wait_recv()
+    exchanged(2, send1, land1).wait_recv()
 
     def unpack(g, carry):
         where = pl.ds(g * group, group)
-        halves = [land1[h, where].astype(F32).reshape(rows4, width).astype(BF) for h in range(2)]
-        out = dot(mix8[...], jnp.concatenate(halves, axis=0), 0, 0).astype(BF)
+        ones = [land1q[q, where].astype(F32).reshape(rows4, lanes).astype(BF) for q in range(2)]
+        split = dot(mixq[0], jnp.concatenate(ones, axis=0), 0, 0)
+        pair = land1[where].astype(F32).reshape(rows4, width).astype(BF)
+        out = dot(mix8[rows4:], pair, 0, 0)
+        out = (out + jnp.concatenate([split[:rows8], split[rows8:]], axis=1)).astype(BF)
         at = pl.ds(pl.multiple_of(g * span, span), span)
         for j in range(nb):
             column[j, at] = out[j * span : (j + 1) * span]
@@ -280,40 +317,48 @@
     for q in range(nb):
         finish(1, q, grad_second)
 
-    for h in range(2):
-        exchanged(1, h, send2, land2).wait_recv()
-
-        def unpack_back(g, carry, h=h):
-            piece = land2[h, pl.ds(g * group, group)].astype(F32).reshape(rows4, width).astype(BF)
+    def under(i, slot):
+        at = pl.ds(i * order, order)
+        dm = dot(pick_t[...], regrouped[slot]).astype(BF)
+        dmixed[slot] = dm
+        term[0, i] = dot(dm, tokens[at, :], 1, 1).astype(BF).reshape(4, part, order)
+        near_own(0, i).start()
+        near_far(0, i).start()
+
+    def down(i, slot):
+        at = pl.ds(i * order, order)
+        inner = dot(block(0, i), dmixed[slot], 0, 0)
+        grad_tokens[at, :] = (inner + spread[at, :]).astype(BF)
+        middle(0, i)
+
+    exchanged(3, send2, land2).wait_recv()
+
+    def unpack_back(g, carry):
+        piece = land2[pl.ds(g * group, group)].astype(F32).reshape(rows4, width).astype(BF)
+        out = dot(mix4[...], piece, 0, 0).astype(BF)
+        at = pl.ds(pl.multiple_of(g * span, span), span)
+        regrouped[0, at] = out[:span]
+        regrouped[1, at] = out[span:]
+        return carry
+
+    lax.fori_loop(0, groups, unpack_back, 0)
+    for i in range(2):
+        under(i, i)
+    for i in range(2):
+        down(i, i)
+    for q in range(2):
+        exchanged(4 + q, send2q.at[q], land2q.at[q]).wait_recv()
+
+        def unpack_one(g, carry, q=q):
+            piece = land2q[q, pl.ds(g * group, group)].astype(F32).reshape(rows4, lanes).astype(BF)
             out = dot(mix4[...], piece, 0, 0).astype(BF)
             at = pl.ds(pl.multiple_of(g * span, span), span)
-            regrouped[0, at] = out[:span]
-            regrouped[1, at] = out[span:]
+            regrouped[q, at] = jnp.concatenate([out[:span], out[span:]], axis=1)
             return carry
 
-        lax.fori_loop(0, groups, unpack_back, 0)
-
-        def under(i2, carry, h=h):
-            i = 2 * h + i2
-            at = pl.ds(pl.multiple_of(i * order, order), order)
-            dm = dot(pick_t[...], regrouped[i2]).astype(BF)
-            dmixed[i2] = dm
-            term[0, i] = dot(dm, tokens[at, :], 1, 1).astype(BF).reshape(4, part, order)
-            near_own(0, i).start()
-            near_far(0, i).start()
-            return carry
-
-        lax.fori_loop(0, 2, under, 0)
-
-        def down(i2, carry, h=h):
-            i = 2 * h + i2
-            at = pl.ds(pl.multiple_of(i * order, order), order)
-            inner = dot(block(0, i), dmixed[i2], 0, 0)
-            grad_tokens[at, :] = (inner + spread[at, :]).astype(BF)
-            middle(0, i)
-            return carry
-
-        lax.fori_loop(0, 2, down, 0)
+        lax.fori_loop(0, groups, unpack_one, 0)
+        under(2 + q, q)
+        down(2 + q, q)
     for q in range(nb):
         finish(0, q, grad_first)
 
@@ -325,9 +370,17 @@
             near_own(f, i).wait_send()
             near_far(f, i).wait_send()
             across(f, i).wait_send()
-    for h in range(2):
-        exchanged(0, h, send1, land1).wait_send()
-        exchanged(1, h, send2, land2).wait_send()
+    for q in range(2):
+        exchanged(q, send1q.at[q], land1q.at[q]).wait_send()
+        exchanged(4 + q, send2q.at[q], land2q.at[q]).wait_send()
+    exchanged(2, send1, land1).wait_send()
+    exchanged(3, send2, land2).wait_send()
+
+
+def hand_over(a, b, c, a_out, b_out, c_out):
+    a_out[...] = a[...]
+    b_out[...] = b[...]
+    c_out[...] = c[...]
 
 
 def solution(mesh):
@@ -345,9 +398,12 @@
                 jax.ShapeDtypeStruct((nb, part, order), BF),
                 jax.ShapeDtypeStruct((nb, part, order), BF),
             ],
-            in_specs=[pl.BlockSpec(memory_space=vmem)] * 6,
+            in_specs=[pl.BlockSpec(memory_space=pl.ANY)] * 4
+            + [pl.BlockSpec(memory_space=vmem)] * 2,
             out_specs=[pl.BlockSpec(memory_space=vmem)] * 3,
             scratch_shapes=[
+                vmem((rows, width), BF),
+                vmem((rows, width), BF),
                 vmem((2, nb, 4, part, order), BF),
                 vmem((width, width), BF),
                 vmem((rows, width), F32),
@@ -357,11 +413,16 @@
                 vmem((order, order), BF),
                 vmem((group * 8, group * 8), BF),
                 vmem((group * 16, group * 16), BF),
+                vmem((2, group * 16, group * 32), BF),
                 vmem((nb, order, width), BF),
-                vmem((2, n, 8, width), BF),
-                vmem((2, n, 8, width), BF),
-                vmem((2, n, 8, width), BF),
-                vmem((2, n, 8, width), BF),
+                vmem((n, 8, width), BF),
+                vmem((n, 8, width), BF),
+                vmem((2, n, 8, width // 2), BF),
+                vmem((2, n, 8, width // 2), BF),
+                vmem((n, 8, width), BF),
+                vmem((n, 8, width), BF),
+                vmem((2, n, 8, width // 2), BF),
+                vmem((2, n, 8, width // 2), BF),
                 vmem((2, order, width), BF),
                 vmem((nb, order, width), BF),
                 vmem((2, order, width), BF),
@@ -371,10 +432,11 @@
                 vmem((2, nb, part, order), BF),
                 pltpu.SemaphoreType.DMA((2, nb, 3)),
                 pltpu.SemaphoreType.DMA((2, nb, 3)),
-                pltpu.SemaphoreType.DMA((2, 2)),
-                pltpu.SemaphoreType.DMA((2, 2)),
+                pltpu.SemaphoreType.DMA((6,)),
+                pltpu.SemaphoreType.DMA((6,)),
                 pltpu.SemaphoreType.DMA((2, nb, 3)),
                 pltpu.SemaphoreType.DMA((2, nb, 3)),
+                pltpu.SemaphoreType.DMA((4,)),
             ],
             compiler_params=pltpu.CompilerParams(
                 collective_id=0, has_side_effects=True, vmem_limit_bytes=56 << 20
@@ -387,6 +449,12 @@
             gate_source.reshape(1, -1),
             alternate.reshape(1, -1),
         )
+        out = pl.pallas_call(
+            hand_over,
+            out_shape=[jax.ShapeDtypeStruct(o.shape, o.dtype) for o in out],
+            in_specs=[pl.BlockSpec(memory_space=vmem)] * 3,
+            out_specs=[pl.BlockSpec(memory_space=vmem)] * 3,
+        )(*out)
         return out[0][None], out[1], out[2]
 
     in_specs = (

time: 146 us -> 136 us (0.932)
  Pallas kernels: 141 us -> 135 us
  local copies, waits for them, and re-layouts: 4.35 us -> 0 us
    pallas_call x1, Pallas kernels: 141 us -> 132 us  [shards(): pl.pallas_call(functools.partial(kernel, n), out_shape=[jax.ShapeDtypeStr...]
    unnamed x7 -> x0, local copies, waits for them, and re-layouts: 4.35 us -> none
    pallas_call x0 -> x1, Pallas kernels: none -> 2.86 us  [shards(): pl.pallas_call(hand_over, out_shape=[jax.ShapeDtypeStruct(o.shape, o.dtyp...]
where the time goes in v2:
time: 136 us
  Pallas kernels  135 us (99%)
    pallas_call x1, Pallas kernels, shards(): pl.pallas_call(functools.partial(kernel, n), out_shape=[jax.ShapeDtypeStr...  132 us
    pallas_call x1, Pallas kernels, shards(): pl.pallas_call(hand_over, out_shape=[jax.ShapeDtypeStruct(o.shape, o.dtyp...  2.86 us

profile of v2, /device:TPU:1, one launch (start us, length us, event | category | flops | bytes accessed | tf_op | source)
XLA Modules:
  0.0 135.6 jit_solution(5111549828062501901)
XLA Ops:
  0.6 132.1 %shard_map.85 = (bf16[2048,256]{1,0:T(8,128)(2,1)}, bf16[4,128,512]{2,1,0:T(8,128)(2,1)}, bf16[4,128,512]{2,1,0:T(8,128)(2,1)}) custom-call(bf16[2048,256]{1,0:T(8,128)(2,1)} %bitcast.5, bf16[2048,256]{1,0:T(8,128)(2,1)} %bitcast.6, bf16[4,128,512]{2,1,0:T(8,128)(2,1)} %first.1, bf16[4,128,512]{2,1,0:T(8,128)(2,1)} %second.1, s32[1,256]{1,0:T(1,128)} %bitcast.8, ...), custom_call_target="tpu_custom_call" | custom-call | tf_op jit(solution)/shard_map/pallas_call | solution.py:394
  132.8 2.9 %shard_map.86 = (bf16[2048,256]{1,0:T(8,128)(2,1)}, bf16[4,128,512]{2,1,0:T(8,128)(2,1)}, bf16[4,128,512]{2,1,0:T(8,128)(2,1)}) custom-call(bf16[2048,256]{1,0:T(8,128)(2,1)} %get-tuple-element.9.a, bf16[4,128,512]{2,1,0:T(8,128)(2,1)} %get-tuple-element.10.b, bf16[4,128,512]{2,1,0:T(8,128)(2,1)} %get-tuple-element.11.c), custom_call_target="tpu_custom_call" | custom-call | tf_op jit(solution)/shard_map/pallas_call | solution.py:452

commit v3 on v2

--- a/solution.py
+++ b/solution.py
@@ -194,7 +194,7 @@
             send1q[i, pl.ds(g * group, group)] = out.reshape(group, 8, lanes).astype(BF)
             return carry
 
-        lax.fori_loop(0, groups, pack_one, 0)
+        lax.fori_loop(0, groups, pack_one, 0, unroll=True)
         exchange(i, send1q.at[i], land1q.at[i])
     for i in (2, 3):
         to_far(0, i).wait_recv()
@@ -347,6 +347,9 @@
     for i in range(2):
         down(i, i)
     for q in range(2):
+        if q == 1:
+            finish(0, 0, grad_first)
+            finish(0, 1, grad_first)
         exchanged(4 + q, send2q.at[q], land2q.at[q]).wait_recv()
 
         def unpack_one(g, carry, q=q):
@@ -356,10 +359,10 @@
             regrouped[q, at] = jnp.concatenate([out[:span], out[span:]], axis=1)
             return carry
 
-        lax.fori_loop(0, groups, unpack_one, 0)
+        lax.fori_loop(0, groups, unpack_one, 0, unroll=True)
         under(2 + q, q)
         down(2 + q, q)
-    for q in range(nb):
+    for q in range(2, nb):
         finish(0, q, grad_first)
 
     for f in range(2):
@@ -377,10 +380,20 @@
     exchanged(3, send2, land2).wait_send()
 
 
-def hand_over(a, b, c, a_out, b_out, c_out):
-    a_out[...] = a[...]
-    b_out[...] = b[...]
-    c_out[...] = c[...]
+def hand_over(a, b, c, a_out, b_out, c_out, a_held, b_held, c_held, got, sent):
+    helds = (a_held, b_held, c_held)
+    ins = [pltpu.make_async_copy(x, held, got.at[q]) for q, (x, held) in enumerate(zip((a, b, c), helds))]
+    outs = [
+        pltpu.make_async_copy(held, x, sent.at[q])
+        for q, (x, held) in enumerate(zip((a_out, b_out, c_out), helds))
+    ]
+    for copy in ins:
+        copy.start()
+    for load, store in zip(ins, outs):
+        load.wait()
+        store.start()
+    for copy in outs:
+        copy.wait()
 
 
 def solution(mesh):
@@ -452,8 +465,11 @@
         out = pl.pallas_call(
             hand_over,
             out_shape=[jax.ShapeDtypeStruct(o.shape, o.dtype) for o in out],
-            in_specs=[pl.BlockSpec(memory_space=vmem)] * 3,
-            out_specs=[pl.BlockSpec(memory_space=vmem)] * 3,
+            in_specs=[pl.BlockSpec(memory_space=pl.ANY)] * 3,
+            out_specs=[pl.BlockSpec(memory_space=pl.ANY)] * 3,
+            scratch_shapes=[vmem(o.shape, o.dtype) for o in out]
+            + [pltpu.SemaphoreType.DMA((3,)), pltpu.SemaphoreType.DMA((3,))],
+            compiler_params=pltpu.CompilerParams(vmem_limit_bytes=56 << 20),
         )(*out)
         return out[0][None], out[1], out[2]
 

time: 136 us -> 134 us (0.985)
  Pallas kernels: 135 us -> 133 us
    pallas_call x1, Pallas kernels: 132 us -> 130 us  [shards(): pl.pallas_call(functools.partial(kernel, n), out_shape=[jax.ShapeDtypeStr...]
where the time goes in v3:
time: 134 us; the launch traced here: 133 us
  Pallas kernels  133 us (99%)
    pallas_call x1, Pallas kernels, shards(): pl.pallas_call(functools.partial(kernel, n), out_shape=[jax.ShapeDtypeStr...  130 us

profile of v3, /device:TPU:1, one launch (start us, length us, event | category | flops | bytes accessed | tf_op | source)
XLA Modules:
  0.0 133.3 jit_solution(8008284207407311321)
XLA Ops:
  0.6 130.1 %shard_map.85 = (bf16[2048,256]{1,0:T(8,128)(2,1)}, bf16[4,128,512]{2,1,0:T(8,128)(2,1)}, bf16[4,128,512]{2,1,0:T(8,128)(2,1)}) custom-call(bf16[2048,256]{1,0:T(8,128)(2,1)} %bitcast.5, bf16[2048,256]{1,0:T(8,128)(2,1)} %bitcast.6, bf16[4,128,512]{2,1,0:T(8,128)(2,1)} %first.1, bf16[4,128,512]{2,1,0:T(8,128)(2,1)} %second.1, s32[1,256]{1,0:T(1,128)} %bitcast.8, ...), custom_call_target="tpu_custom_call" | custom-call | tf_op jit(solution)/shard_map/pallas_call | solution.py:407
  130.7 2.6 %shard_map.86 = (bf16[2048,256]{1,0:T(8,128)(2,1)}, bf16[4,128,512]{2,1,0:T(8,128)(2,1)}, bf16[4,128,512]{2,1,0:T(8,128)(2,1)}) custom-call(bf16[2048,256]{1,0:T(8,128)(2,1)} %get-tuple-element.9.a, bf16[4,128,512]{2,1,0:T(8,128)(2,1)} %get-tuple-element.10.b, bf16[4,128,512]{2,1,0:T(8,128)(2,1)} %get-tuple-element.11.c), custom_call_target="tpu_custom_call" | custom-call | tf_op jit(solution)/shard_map/pallas_call | solution.py:465
